TPU v7x, 32 devices: a whole 2x2x4 slice. The times are simulated.
32 devices in a mesh: gz: 8 (over z, y), xy: 4 (over x, core).
Axes of the slice: x: 2, y: 2, z: 4, core: 2. Of those that a mesh axis runs over, the one named last changes fastest.
Arguments:
- volume: float32 [128, 128, 128], P('gz', 'xy'), may hold values from -6 to 6
- owners: int32 [4, 32, 1], P('xy', 'gz'), may hold values from 0 to 7; in each aligned block of 4 rows (0 to 3, 4 to 7, ..., all dimensions but the last counted through in order) at most 2 rows name the same one
Outputs:
- denoised: float32 [128, 128, 128], P('gz', 'xy')
- routed: float32 [4, 128, 128, 128], P('xy', 'gz')
Inputs may be any that keep to these rules, and one draw needn't show every extreme that they name: `owners`: among the 4 blocks of one device no destination is named more than 2 times, a bound that some block reaches.
All inputs are finite; a program needn't handle non-finite values.
Results may differ from a plain program's by a relative error of at most 0.0003.
Values sent between devices are 32-bit elements; how exact they have to be, the bound alone decides.
No kernel may reach another device: no remote copies, remote signals or barrier semaphores. Data moves between devices by JAX's collectives and lax.ppermute only.
A program may use at most 64 MiB of HBM per device.

v0:
```python
import jax
import jax.numpy as jnp
from jax import lax
from jax.sharding import PartitionSpec as P

STEPS = 2
MOST = 2
BLOCK_ROWS = 128
TIME_STEP = 30.0
CONTRAST = 4.0


def with_halo(block, sides, width):
    for axis, dim in sides:
        count = lax.axis_size(axis)
        forward = [(i, i + 1) for i in range(count - 1)]
        backward = [(target, source) for source, target in forward]
        low = lax.ppermute(
            lax.slice_in_dim(block, block.shape[dim] - width, None, axis=dim), axis, forward
        )
        high = lax.ppermute(lax.slice_in_dim(block, 0, width, axis=dim), axis, backward)
        block = jnp.concatenate([low, block, high], axis=dim)
    return block


def shifted(field, stride, line_axis, fill, before):
    length = field.shape[line_axis]
    shape = list(field.shape)
    shape[line_axis] = stride
    padding = jnp.full(tuple(shape), fill, field.dtype)
    if before:
        return jnp.concatenate(
            [padding, lax.slice_in_dim(field, 0, length - stride, axis=line_axis)], axis=line_axis
        )
    return jnp.concatenate(
        [lax.slice_in_dim(field, stride, length, axis=line_axis), padding], axis=line_axis
    )


def cyclic_solve(low_diag, main_diag, high_diag, right_side, line_axis, side_axis):
    length = main_diag.shape[line_axis]
    stride = 1
    while stride < length:
        low_prev = shifted(low_diag, stride, line_axis, 0.0, True)
        main_prev = shifted(main_diag, stride, line_axis, 1.0, True)
        high_prev = shifted(high_diag, stride, line_axis, 0.0, True)
        side_prev = shifted(right_side, stride, side_axis, 0.0, True)
        low_next = shifted(low_diag, stride, line_axis, 0.0, False)
        main_next = shifted(main_diag, stride, line_axis, 1.0, False)
        high_next = shifted(high_diag, stride, line_axis, 0.0, False)
        side_next = shifted(right_side, stride, side_axis, 0.0, False)
        factor_low = -low_diag / main_prev
        factor_high = -high_diag / main_next
        main_diag = main_diag + factor_low * high_prev + factor_high * low_next
        right_side = right_side + factor_low * side_prev + factor_high * side_next
        low_diag = factor_low * low_prev
        high_diag = factor_high * high_next
        stride = stride * 2
    return right_side / main_diag


def coefficients(g_line, line_axis, has_before, has_after):
    length = g_line.shape[line_axis] - 2
    weight = 0.5 * (
        lax.slice_in_dim(g_line, 0, length + 1, axis=line_axis)
        + lax.slice_in_dim(g_line, 1, length + 2, axis=line_axis)
    )
    shape = [1] * weight.ndim
    shape[line_axis] = length + 1
    edge_index = lax.broadcasted_iota(jnp.int32, tuple(shape), line_axis)
    keep_mask = jnp.where(edge_index == 0, has_before, 1.0) * jnp.where(
        edge_index == length, has_after, 1.0
    )
    weight = weight * keep_mask
    low_diag = -3.0 * TIME_STEP * lax.slice_in_dim(weight, 0, length, axis=line_axis)
    high_diag = -3.0 * TIME_STEP * lax.slice_in_dim(weight, 1, length + 1, axis=line_axis)
    main_diag = 1.0 - low_diag - high_diag
    return (low_diag, main_diag, high_diag)


def pad_zero(field, line_axis):
    widths = [(0, 0)] * field.ndim
    widths[line_axis] = (1, 1)
    return jnp.pad(field, widths)


def diffusivity(extended, z_start, z_total, y_start, y_total):
    center = extended[1:-1, 1:-1]
    z_index = z_start - 1 + lax.broadcasted_iota(jnp.int32, (center.shape[0], 1, 1), 0)
    z_next = jnp.where(z_index + 1 < z_total, extended[2:, 1:-1], center)
    z_prev = jnp.where(z_index >= 1, extended[:-2, 1:-1], center)
    y_index = y_start - 1 + lax.broadcasted_iota(jnp.int32, (1, center.shape[1], 1), 1)
    y_next = jnp.where(y_index + 1 < y_total, extended[1:-1, 2:], center)
    y_prev = jnp.where(y_index >= 1, extended[1:-1, :-2], center)
    x_next = jnp.concatenate([center[:, :, 1:], center[:, :, -1:]], axis=2)
    x_prev = jnp.concatenate([center[:, :, :1], center[:, :, :-1]], axis=2)
    slope_z = (z_next - z_prev) * 0.5
    slope_y = (y_next - y_prev) * 0.5
    slope_x = (x_next - x_prev) * 0.5
    squares = slope_z * slope_z + slope_y * slope_y + slope_x * slope_x
    return 1.0 / (1.0 + squares / CONTRAST)


def line_solve(g_field, right_side, line_axis):
    low_diag, main_diag, high_diag = coefficients(pad_zero(g_field, line_axis), line_axis, 0.0, 0.0)
    return cyclic_solve(low_diag, main_diag, high_diag, right_side, line_axis, line_axis)


def interface_solve(gathered, position, chain_size):
    parts = tuple((gathered[:, k] for k in range(6)))
    zeros = jnp.zeros_like(parts[0][0])

    def forward(carry, item):
        prev_p, prev_q = carry
        head_y, head_v, head_w, tail_y, tail_v, tail_w = item
        denom = 1.0 - head_v * prev_q
        first_r = (head_y + head_v * prev_p) / denom
        first_s = head_w / denom
        new_p = tail_y + tail_v * (prev_p + prev_q * first_r)
        new_q = tail_v * prev_q * first_s + tail_w
        return ((new_p, new_q), (first_r, first_s, new_p, new_q))

    carry_out, sweep = lax.scan(forward, (zeros, zeros), parts)

    def backward(later_f, item):
        first_r, first_s, new_p, new_q = item
        head_value = first_r + first_s * later_f
        return (head_value, (head_value, new_p + new_q * later_f))

    final_f, (head_values, tail_values) = lax.scan(backward, zeros, sweep, reverse=True)
    left_pick = lax.dynamic_index_in_dim(
        tail_values, jnp.maximum(position - 1, 0), 0, keepdims=False
    )
    right_pick = lax.dynamic_index_in_dim(
        head_values, jnp.minimum(position + 1, chain_size - 1), 0, keepdims=False
    )
    left_value = jnp.where(position > 0, left_pick, 0.0)
    right_value = jnp.where(position < chain_size - 1, right_pick, 0.0)
    return (left_value, right_value)


def split_solve(g_line, right_side, line_axis, position, chain_size, gather_links):
    has_before = (position > 0).astype(jnp.float32)
    has_after = (position < chain_size - 1).astype(jnp.float32)
    low_diag, main_diag, high_diag = coefficients(g_line, line_axis, has_before, has_after)
    length = main_diag.shape[line_axis]
    shape = [1] * 3
    shape[line_axis] = length
    cell_index = lax.broadcasted_iota(jnp.int32, tuple(shape), line_axis)
    first_link = lax.slice_in_dim(low_diag, 0, 1, axis=line_axis)
    last_link = lax.slice_in_dim(high_diag, length - 1, length, axis=line_axis)
    low_local = jnp.where(cell_index == 0, 0.0, low_diag)
    high_local = jnp.where(cell_index == length - 1, 0.0, high_diag)
    left_side = jnp.where(cell_index == 0, -first_link, 0.0)
    right_part = jnp.where(cell_index == length - 1, -last_link, 0.0)
    stacked = jnp.stack([right_side, left_side, right_part])
    solved = cyclic_solve(low_local, main_diag, high_local, stacked, line_axis, line_axis + 1)
    head = lax.index_in_dim(solved, 0, line_axis + 1, keepdims=False)
    tail = lax.index_in_dim(solved, length - 1, line_axis + 1, keepdims=False)
    packed = jnp.concatenate([head, tail], axis=0)
    gathered = gather_links(packed[None])
    left_value, right_value = interface_solve(gathered, position, chain_size)
    return (
        solved[0]
        + solved[1] * jnp.expand_dims(left_value, line_axis)
        + solved[2] * jnp.expand_dims(right_value, line_axis)
    )


def gather_y(packed):
    return lax.all_gather(packed, "xy", axis=0, tiled=True)


def on_device(volume, owners):
    field = volume
    depth, height, width = field.shape
    z_rank = lax.axis_index("gz")
    z_count = lax.axis_size("gz")
    y_rank = lax.axis_index("xy")
    y_count = lax.axis_size("xy")
    for section_index in range(STEPS):
        extended = with_halo(field, (("gz", 0), ("xy", 1)), 2)
        g_ext = diffusivity(
            extended, z_rank * depth, depth * z_count, y_rank * height, height * y_count
        )
        g_own = g_ext[1:-1, 1:-1]
        along_x = line_solve(g_own, field, 2)
        along_y = split_solve(g_ext[1:-1], field, 1, y_rank, y_count, gather_y)
        moved_g, moved_field = (
            lax.all_to_all(g_own, "gz", split_axis=1, concat_axis=0, tiled=True),
            lax.all_to_all(field, "gz", split_axis=1, concat_axis=0, tiled=True),
        )
        along_z = lax.all_to_all(
            line_solve(moved_g, moved_field, 0), "gz", split_axis=0, concat_axis=1, tiled=True
        )
        field = (along_x + along_y + along_z) / 3.0
    blocks = field.reshape(-1, BLOCK_ROWS, width)
    targets = owners.reshape(-1)
    block_count = targets.shape[0]
    same = targets[:, None] == targets[None, :]
    block_iota = jnp.arange(block_count, dtype=jnp.int32)
    earlier = block_iota[:, None] < block_iota[None, :]
    order_rank = jnp.sum((same & earlier).astype(jnp.int32), axis=0)
    slot_index = targets * MOST + order_rank
    outgoing = (
        jnp.zeros((z_count * MOST, BLOCK_ROWS, width), field.dtype).at[slot_index].set(blocks)
    )
    incoming = lax.all_to_all(outgoing, "gz", split_axis=0, concat_axis=0, tiled=True)
    return (field, incoming.reshape(1, z_count * MOST, BLOCK_ROWS, width))


def solution(mesh):
    in_specs = (P("gz", "xy", None), P("xy", "gz", None))
    out_specs = (P("gz", "xy", None), P("xy", "gz", None, None))
    return jax.shard_map(
        on_device, mesh=mesh, in_specs=in_specs, out_specs=out_specs, check_vma=False
    )
```

profile of v0, /device:TPU:0, one launch (start us, length us, event | category | flops | bytes accessed | tf_op | source)
XLA Modules:
  0.0 191.8 jit_solution(1808513915157954361)
XLA Ops:
  0.6 1.8 copy.129
  2.4 7.3 %all-to-all-start = ((f32[16,32,128]{2,0,1:T(8,128)}), f32[16,32,128]{2,0,1:T(8,128)S(1)}, u32[]{:S(2)}, u32[]{:S(2)}) async-start(f32[16,32,128]{2,0,1:T(8,128)} %copy.129), calls=%async_computation | async-start | bytes 524288 | tf_op jit(solution)/shard_map/all_to_all | solution.py:191
  10.8 1.3 collective-permute-start.1
  12.1 4.6 %collective-permute-start = (f32[2,32,128]{2,0,1:T(2,128)S(1)}, f32[2,32,128]{2,0,1:T(2,128)S(1)}, u32[]{:S(2)}, u32[]{:S(2)}) collective-permute-start(f32[2,32,128]{2,0,1:T(2,128)S(1)} %get-tuple-element.1167), channel_id=1, source_target_pairs={{0,4},{4,8},{8,12},{12,16},{16,20},{20,24},{24,28},{1,5},{5,9},{9,... | collective-permute-start | bytes 98312 | tf_op jit(solution)/shard_map/ppermute | solution.py:18
  16.6 1.2 fusion.185
  19.4 1.3 collective-permute-start.2
  20.7 1.3 collective-permute-start.3
  22.0 3.5 %collective-permute-done.3 = f32[20,2,128]{2,0,1:T(8,128)S(1)} collective-permute-done((f32[20,2,128]{2,0,1:T(8,128)S(1)}, f32[20,2,128]{2,0,1:T(8,128)S(1)}, u32[]{:S(2)}, u32[]{:S(2)}) %collective-permute-start.3) | collective-permute-done | bytes 20512 | tf_op jit(solution)/shard_map/ppermute | solution.py:21
  26.9 1.6 fusion.39
  29.7 1.2 fusion.15
  41.8 6.8 %all-gather = f32[24,16,128]{2,1,0:T(8,128)S(1)} all-gather(f32[6,16,128]{2,1,0:T(8,128)S(1)} %pad_maximum_fusion.16), channel_id=2, replica_groups=mesh['gz'=8,'xy'=4] {'xy'}, dimensions={0}, use_global_device_ids=true | all-gather | bytes 245760 | tf_op jit(solution)/shard_map/all_gather | solution.py:171
  49.1 7.3 %all-to-all-start.1 = ((f32[16,32,128]{2,0,1:T(8,128)}), f32[16,32,128]{2,0,1:T(8,128)S(1)}, u32[]{:S(2)}, u32[]{:S(2)}) async-start(f32[16,32,128]{2,0,1:T(8,128)} %slice.1507), calls=%async_computation.1 | async-start | bytes 524288 | tf_op jit(solution)/shard_map/all_to_all | solution.py:190
  56.5 9.1 %all-to-all-done.1 = f32[16,32,128]{2,0,1:T(8,128)S(1)} async-done(((f32[16,32,128]{2,0,1:T(8,128)}), f32[16,32,128]{2,0,1:T(8,128)S(1)}, u32[]{:S(2)}, u32[]{:S(2)}) %all-to-all-start.1) | async-done | bytes 262176 | tf_op jit(solution)/shard_map/all_to_all | solution.py:190
  69.9 3.6 %all-to-all-start.2 = ((f32[128,4,128]{2,1,0:T(4,128)}), f32[128,4,128]{2,1,0:T(4,128)S(1)}, u32[]{:S(2)}, u32[]{:S(2)}) async-start(f32[128,4,128]{2,1,0:T(4,128)} %copy.142), calls=%async_computation.2 | async-start | bytes 524288 | tf_op jit(solution)/shard_map/all_to_all | solution.py:193
  74.5 7.6 %all-to-all-done.2 = f32[128,4,128]{2,1,0:T(4,128)S(1)} async-done(((f32[128,4,128]{2,1,0:T(4,128)}), f32[128,4,128]{2,1,0:T(4,128)S(1)}, u32[]{:S(2)}, u32[]{:S(2)}) %all-to-all-start.2) | async-done | bytes 262176 | tf_op jit(solution)/shard_map/all_to_all | solution.py:193
  85.1 1.3 collective-permute-start.5
  86.4 4.5 %collective-permute-start.4 = (f32[2,32,128]{2,0,1:T(2,128)S(1)}, f32[2,32,128]{2,0,1:T(2,128)S(1)}, u32[]{:S(2)}, u32[]{:S(2)}) collective-permute-start(f32[2,32,128]{2,0,1:T(2,128)S(1)} %get-tuple-element.1035), channel_id=1, source_target_pairs={{0,4},{4,8},{8,12},{12,16},{16,20},{20,24},{24,28},{1,5},{5,9},{9,... | collective-permute-start | bytes 98312 | tf_op jit(solution)/shard_map/ppermute | solution.py:18
  91.0 3.7 %all-to-all-start.3 = ((f32[16,32,128]{2,0,1:T(8,128)}), f32[16,32,128]{2,0,1:T(8,128)S(1)}, u32[]{:S(2)}, u32[]{:S(2)}) async-start(f32[16,32,128]{2,0,1:T(8,128)} %fusion.61), calls=%async_computation.3 | async-start | bytes 524288 | tf_op jit(solution)/shard_map/all_to_all | solution.py:191
  95.4 1.3 collective-permute-start.6
  96.7 1.3 collective-permute-start.7
  98.0 1.2 fusion.119
  99.2 2.7 %collective-permute-done.7 = f32[20,2,128]{2,0,1:T(8,128)S(1)} collective-permute-done((f32[20,2,128]{2,0,1:T(8,128)S(1)}, f32[20,2,128]{2,0,1:T(8,128)S(1)}, u32[]{:S(2)}, u32[]{:S(2)}) %collective-permute-start.7) | collective-permute-done | bytes 20512 | tf_op jit(solution)/shard_map/ppermute | solution.py:21
  103.3 1.6 fusion.26
  107.5 1.2 multiply_add_fusion.3
  110.9 1.2 fusion.17
  112.7 1.3 multiply_add_fusion.35
  120.2 6.8 %all-gather.1 = f32[24,16,128]{2,1,0:T(8,128)S(1)} all-gather(f32[6,16,128]{2,1,0:T(8,128)S(1)} %pad_maximum_fusion.17), channel_id=3, replica_groups=mesh['gz'=8,'xy'=4] {'xy'}, dimensions={0}, use_global_device_ids=true | all-gather | bytes 245760 | tf_op jit(solution)/shard_map/all_gather | solution.py:171
  127.5 6.0 %all-to-all-start.4 = ((f32[16,32,128]{2,0,1:T(8,128)}), f32[16,32,128]{2,0,1:T(8,128)S(1)}, u32[]{:S(2)}, u32[]{:S(2)}) async-start(f32[16,32,128]{2,0,1:T(8,128)} %slice.1684), calls=%async_computation.4 | async-start | bytes 524288 | tf_op jit(solution)/shard_map/all_to_all | solution.py:190
  133.6 9.1 %all-to-all-done.4 = f32[16,32,128]{2,0,1:T(8,128)S(1)} async-done(((f32[16,32,128]{2,0,1:T(8,128)}), f32[16,32,128]{2,0,1:T(8,128)S(1)}, u32[]{:S(2)}, u32[]{:S(2)}) %all-to-all-start.4) | async-done | bytes 262176 | tf_op jit(solution)/shard_map/all_to_all | solution.py:190
  147.0 3.6 %all-to-all-start.5 = ((f32[128,4,128]{2,1,0:T(4,128)}), f32[128,4,128]{2,1,0:T(4,128)S(1)}, u32[]{:S(2)}, u32[]{:S(2)}) async-start(f32[128,4,128]{2,1,0:T(4,128)} %copy.154), calls=%async_computation.5 | async-start | bytes 524288 | tf_op jit(solution)/shard_map/all_to_all | solution.py:193
  151.6 7.5 %all-to-all-done.5 = f32[128,4,128]{2,1,0:T(4,128)S(1)} async-done(((f32[128,4,128]{2,1,0:T(4,128)}), f32[128,4,128]{2,1,0:T(4,128)S(1)}, u32[]{:S(2)}, u32[]{:S(2)}) %all-to-all-start.5) | async-done | bytes 262176 | tf_op jit(solution)/shard_map/all_to_all | solution.py:193
  162.0 28.8 %all_to_all.113 = f32[16,128,128]{2,1,0:T(8,128)S(1)} all-to-all(f32[16,128,128]{2,1,0:T(8,128)S(1)} %scatter_fusion), channel_id=1, replica_groups=mesh['gz'=8,'xy'=4] {'gz'}, dimensions={0} | all-to-all | bytes 2097152 | tf_op jit(solution)/shard_map/all_to_all | solution.py:208
  (351 shorter events, 46.4 us)
Async XLA Ops:
  2.4 46.6 %all-to-all-start = ((f32[16,32,128]{2,0,1:T(8,128)}), f32[16,32,128]{2,0,1:T(8,128)S(1)}, u32[]{:S(2)}, u32[]{:S(2)}) async-start(f32[16,32,128]{2,0,1:T(8,128)} %copy.129), calls=%async_computation | async-start | bytes 524288 | tf_op jit(solution)/shard_map/all_to_all | solution.py:191
  10.8 7.8 %collective-permute-start.1 = (f32[2,32,128]{2,0,1:T(2,128)S(1)}, f32[2,32,128]{2,0,1:T(2,128)S(1)}, u32[]{:S(2)}, u32[]{:S(2)}) collective-permute-start(f32[2,32,128]{2,0,1:T(2,128)S(1)} %get-tuple-element.1168), channel_id=1, source_target_pairs={{4,0},{8,4},{12,8},{16,12},{20,16},{24,20},{28,24},{5,1},{9,5},{13... | collective-permute-start | bytes 98312 | tf_op jit(solution)/shard_map/ppermute | solution.py:21
  12.1 6.6 %collective-permute-start = (f32[2,32,128]{2,0,1:T(2,128)S(1)}, f32[2,32,128]{2,0,1:T(2,128)S(1)}, u32[]{:S(2)}, u32[]{:S(2)}) collective-permute-start(f32[2,32,128]{2,0,1:T(2,128)S(1)} %get-tuple-element.1167), channel_id=1, source_target_pairs={{0,4},{4,8},{8,12},{12,16},{16,20},{20,24},{24,28},{1,5},{5,9},{9,... | collective-permute-start | bytes 98312 | tf_op jit(solution)/shard_map/ppermute | solution.py:18
  17.8 0.7 copy-start.5
  19.4 2.7 %collective-permute-start.2 = (f32[20,2,128]{2,0,1:T(8,128)S(1)}, f32[20,2,128]{2,0,1:T(8,128)S(1)}, u32[]{:S(2)}, u32[]{:S(2)}) collective-permute-start(f32[20,2,128]{2,0,1:T(8,128)S(1)} %get-tuple-element.887), channel_id=1, source_target_pairs={{0,1},{1,2},{2,3},{4,5},{5,6},{6,7},{8,9},{9,10},{10,11},{12,13},{... | collective-permute-start | bytes 61448 | tf_op jit(solution)/shard_map/ppermute | solution.py:18
  20.7 4.8 %collective-permute-start.3 = (f32[20,2,128]{2,0,1:T(8,128)S(1)}, f32[20,2,128]{2,0,1:T(8,128)S(1)}, u32[]{:S(2)}, u32[]{:S(2)}) collective-permute-start(f32[20,2,128]{2,0,1:T(8,128)S(1)} %get-tuple-element.886), channel_id=1, source_target_pairs={{1,0},{2,1},{3,2},{5,4},{6,5},{7,6},{9,8},{10,9},{11,10},{13,12},{... | collective-permute-start | bytes 61448 | tf_op jit(solution)/shard_map/ppermute | solution.py:21
  31.4 1.0 copy-start.1
  49.1 16.6 %all-to-all-start.1 = ((f32[16,32,128]{2,0,1:T(8,128)}), f32[16,32,128]{2,0,1:T(8,128)S(1)}, u32[]{:S(2)}, u32[]{:S(2)}) async-start(f32[16,32,128]{2,0,1:T(8,128)} %slice.1507), calls=%async_computation.1 | async-start | bytes 524288 | tf_op jit(solution)/shard_map/all_to_all | solution.py:190
  69.9 12.2 %all-to-all-start.2 = ((f32[128,4,128]{2,1,0:T(4,128)}), f32[128,4,128]{2,1,0:T(4,128)S(1)}, u32[]{:S(2)}, u32[]{:S(2)}) async-start(f32[128,4,128]{2,1,0:T(4,128)} %copy.142), calls=%async_computation.2 | async-start | bytes 524288 | tf_op jit(solution)/shard_map/all_to_all | solution.py:193
  82.1 1.0 copy-start.2
  85.1 9.6 %collective-permute-start.5 = (f32[2,32,128]{2,0,1:T(2,128)S(1)}, f32[2,32,128]{2,0,1:T(2,128)S(1)}, u32[]{:S(2)}, u32[]{:S(2)}) collective-permute-start(f32[2,32,128]{2,0,1:T(2,128)S(1)} %get-tuple-element.1036), channel_id=1, source_target_pairs={{4,0},{8,4},{12,8},{16,12},{20,16},{24,20},{28,24},{5,1},{9,5},{13... | collective-permute-start | bytes 98312 | tf_op jit(solution)/shard_map/ppermute | solution.py:21
  86.4 8.3 %collective-permute-start.4 = (f32[2,32,128]{2,0,1:T(2,128)S(1)}, f32[2,32,128]{2,0,1:T(2,128)S(1)}, u32[]{:S(2)}, u32[]{:S(2)}) collective-permute-start(f32[2,32,128]{2,0,1:T(2,128)S(1)} %get-tuple-element.1035), channel_id=1, source_target_pairs={{0,4},{4,8},{8,12},{12,16},{16,20},{20,24},{24,28},{1,5},{5,9},{9,... | collective-permute-start | bytes 98312 | tf_op jit(solution)/shard_map/ppermute | solution.py:18
  91.0 36.5 %all-to-all-start.3 = ((f32[16,32,128]{2,0,1:T(8,128)}), f32[16,32,128]{2,0,1:T(8,128)S(1)}, u32[]{:S(2)}, u32[]{:S(2)}) async-start(f32[16,32,128]{2,0,1:T(8,128)} %fusion.61), calls=%async_computation.3 | async-start | bytes 524288 | tf_op jit(solution)/shard_map/all_to_all | solution.py:191
  95.4 3.8 %collective-permute-start.6 = (f32[20,2,128]{2,0,1:T(8,128)S(1)}, f32[20,2,128]{2,0,1:T(8,128)S(1)}, u32[]{:S(2)}, u32[]{:S(2)}) collective-permute-start(f32[20,2,128]{2,0,1:T(8,128)S(1)} %get-tuple-element.885), channel_id=1, source_target_pairs={{0,1},{1,2},{2,3},{4,5},{5,6},{6,7},{8,9},{9,10},{10,11},{12,13},{... | collective-permute-start | bytes 61448 | tf_op jit(solution)/shard_map/ppermute | solution.py:18
  96.7 5.2 %collective-permute-start.7 = (f32[20,2,128]{2,0,1:T(8,128)S(1)}, f32[20,2,128]{2,0,1:T(8,128)S(1)}, u32[]{:S(2)}, u32[]{:S(2)}) collective-permute-start(f32[20,2,128]{2,0,1:T(8,128)S(1)} %get-tuple-element.884), channel_id=1, source_target_pairs={{1,0},{2,1},{3,2},{5,4},{6,5},{7,6},{9,8},{10,9},{11,10},{13,12},{... | collective-permute-start | bytes 61448 | tf_op jit(solution)/shard_map/ppermute | solution.py:21
  127.5 15.2 %all-to-all-start.4 = ((f32[16,32,128]{2,0,1:T(8,128)}), f32[16,32,128]{2,0,1:T(8,128)S(1)}, u32[]{:S(2)}, u32[]{:S(2)}) async-start(f32[16,32,128]{2,0,1:T(8,128)} %slice.1684), calls=%async_computation.4 | async-start | bytes 524288 | tf_op jit(solution)/shard_map/all_to_all | solution.py:190
  147.0 12.2 %all-to-all-start.5 = ((f32[128,4,128]{2,1,0:T(4,128)}), f32[128,4,128]{2,1,0:T(4,128)S(1)}, u32[]{:S(2)}, u32[]{:S(2)}) async-start(f32[128,4,128]{2,1,0:T(4,128)} %copy.154), calls=%async_computation.5 | async-start | bytes 524288 | tf_op jit(solution)/shard_map/all_to_all | solution.py:193
  159.2 1.0 copy-start.3
  159.2 1.0 copy-start.4
  160.6 0.7 copy-start
where the time goes:
time: 193 us; the launch traced here: 192 us
  starting transfers between devices  48.3 us (25%)
  blocking collectives  42.4 us (22%)
  waiting for transfers between devices  39.6 us (21%)
  other arithmetic  30.1 us (16%)
  local copies, waits for them, and re-layouts  28 us (15%)
  between operations  2.95 us (2%)
    all_to_all x1, blocking collectives, on_device(): lax.all_to_all(outgoing, 'gz', split_axis=0, concat_axis=0, tiled=True)  28.8 us
    all_to_all x2, waiting for transfers between devices, on_device(): lax.all_to_all(g_own, 'gz', split_axis=1, concat_axis=0, tiled=True)  18.3 us
    all_to_all x2, waiting for transfers between devices, on_device(): lax.all_to_all(line_solve(moved_g, moved_field, 0), 'gz', split_axis=0, c...  15.1 us
    all_gather x2, blocking collectives, gather_y(): return lax.all_gather(packed, 'xy', axis=0, tiled=True)  13.7 us
    all_to_all x2, starting transfers between devices, on_device(): lax.all_to_all(g_own, 'gz', split_axis=1, concat_axis=0, tiled=True)  13.3 us
    ppermute x4, starting transfers between devices, with_halo(): lax.ppermute(lax.slice_in_dim(block, block.shape[dim] - width, None, axis...  11.7 us
    all_to_all x2, starting transfers between devices, on_device(): lax.all_to_all(field, 'gz', split_axis=1, concat_axis=0, tiled=True)  11 us
    slice x82, local copies, waits for them, and re-layouts, shifted(): lax.slice_in_dim(field, 0, length - stride, axis=line_axis)  9.39 us
  transfers between devices with their start and end apart: 14, of which 6 were waited for; matrix products, arithmetic and copies ran while one was open for 21% of the time, Pallas kernels for 0%

commit v1 on v0

--- a/solution.py
+++ b/solution.py
@@ -8,6 +8,11 @@
 BLOCK_ROWS = 128
 TIME_STEP = 30.0
 CONTRAST = 4.0
+
+
+def swapped_in(x, mesh_axis, d):
+    sent = jnp.stack([x] * lax.axis_size(mesh_axis))
+    return jnp.concatenate(lax.all_to_all(sent, mesh_axis, 0, 0), axis=d)
 
 
 def with_halo(block, sides, width):
@@ -168,7 +173,7 @@
 
 
 def gather_y(packed):
-    return lax.all_gather(packed, "xy", axis=0, tiled=True)
+    return swapped_in(packed, "xy", 0)
 
 
 def on_device(volume, owners):

time: 193 us -> 215 us (1.11)
  waiting for transfers between devices: 39.6 us -> 64.4 us
  blocking collectives: 42.4 us -> 28.7 us
  local copies, waits for them, and re-layouts: 28 us -> 31.6 us
  starting transfers between devices: 48.3 us -> 51.8 us
  other arithmetic: 30.1 us -> 33.1 us
    all_to_all x2, waiting for transfers between devices: 0.01 us -> 15.3 us  [on_device(): lax.all_to_all(field, 'gz', split_axis=1, concat_axis=0, tiled=True)]
    all_gather x2 -> x0, blocking collectives: 13.7 us -> none  [gather_y(): return lax.all_gather(packed, 'xy', axis=0, tiled=True)]
    all_to_all x0 -> x2, waiting for transfers between devices: none -> 8.94 us  [swapped_in(): return jnp.concatenate(lax.all_to_all(sent, mesh_axis, 0, 0), axis=d)]
    all_to_all x0 -> x2, starting transfers between devices: none -> 7.65 us  [swapped_in(): return jnp.concatenate(lax.all_to_all(sent, mesh_axis, 0, 0), axis=d)]
    all_to_all x2, starting transfers between devices: 13.3 us -> 7.23 us  [on_device(): lax.all_to_all(g_own, 'gz', split_axis=1, concat_axis=0, tiled=True)]
    all_to_all x2, waiting for transfers between devices: 18.3 us -> 16.1 us  [on_device(): lax.all_to_all(g_own, 'gz', split_axis=1, concat_axis=0, tiled=True)]
    unnamed x15 -> x47, local copies, waits for them, and re-layouts: 6.83 us -> 7.62 us
  transfers between devices with their start and end apart: 14 -> 16, of which waited for: 6 -> 11; matrix products, arithmetic and copies ran while one was open for 21% -> 4% of each run, Pallas kernels for 0% -> 0%
where the time goes in v1:
time: 215 us; the launch traced here: 213 us
  waiting for transfers between devices  64.4 us (30%)
  starting transfers between devices  51.8 us (24%)
  other arithmetic  33.1 us (15%)
  local copies, waits for them, and re-layouts  31.6 us (15%)
  blocking collectives  28.7 us (13%)
  between operations  3.09 us (1%)
    all_to_all x1, blocking collectives, on_device(): lax.all_to_all(outgoing, 'gz', split_axis=0, concat_axis=0, tiled=True)  28.7 us
    all_to_all x2, waiting for transfers between devices, on_device(): lax.all_to_all(line_solve(moved_g, moved_field, 0), 'gz', split_axis=0, c...  16.6 us
    all_to_all x2, waiting for transfers between devices, on_device(): lax.all_to_all(g_own, 'gz', split_axis=1, concat_axis=0, tiled=True)  16.1 us
    all_to_all x2, waiting for transfers between devices, on_device(): lax.all_to_all(field, 'gz', split_axis=1, concat_axis=0, tiled=True)  15.3 us
    ppermute x4, starting transfers between devices, with_halo(): lax.ppermute(lax.slice_in_dim(block, block.shape[dim] - width, None, axis...  12.8 us
    all_to_all x2, starting transfers between devices, on_device(): lax.all_to_all(field, 'gz', split_axis=1, concat_axis=0, tiled=True)  11.8 us
    slice x82, local copies, waits for them, and re-layouts, shifted(): lax.slice_in_dim(field, 0, length - stride, axis=line_axis)  10.9 us
    all_to_all x2, waiting for transfers between devices, swapped_in(): return jnp.concatenate(lax.all_to_all(sent, mesh_axis, 0, 0), axis=d)  8.94 us
  transfers between devices with their start and end apart: 16, of which 11 were waited for; matrix products, arithmetic and copies ran while one was open for 4% of the time, Pallas kernels for 0%

profile of v1, /device:TPU:0, one launch (start us, length us, event | category | flops | bytes accessed | tf_op | source)
XLA Modules:
  0.0 213.2 jit_solution(2333308066686365730)
XLA Ops:
  0.6 1.8 copy.69
  3.4 1.3 collective-permute-start.1
  4.7 5.5 %collective-permute-start = (f32[2,32,128]{2,0,1:T(2,128)S(1)}, f32[2,32,128]{2,0,1:T(2,128)S(1)}, u32[]{:S(2)}, u32[]{:S(2)}) collective-permute-start(f32[2,32,128]{2,0,1:T(2,128)S(1)} %get-tuple-element.1167), channel_id=1, source_target_pairs={{0,4},{4,8},{8,12},{12,16},{16,20},{20,24},{24,28},{1,5},{5,9},{9,... | collective-permute-start | bytes 98312 | tf_op jit(solution)/shard_map/ppermute | solution.py:23
  13.7 1.5 collective-permute-start.2
  15.1 1.3 collective-permute-start.3
  16.5 3.8 %collective-permute-done.3 = f32[20,2,128]{2,0,1:T(8,128)S(1)} collective-permute-done((f32[20,2,128]{2,0,1:T(8,128)S(1)}, f32[20,2,128]{2,0,1:T(8,128)S(1)}, u32[]{:S(2)}, u32[]{:S(2)}) %collective-permute-start.3) | collective-permute-done | bytes 20512 | tf_op jit(solution)/shard_map/ppermute | solution.py:26
  21.7 1.7 fusion.39
  37.3 3.8 %all-to-all-start = ((f32[4,1,6,16,128]{4,3,2,1,0:T(8,128)}), f32[4,1,6,16,128]{4,3,2,1,0:T(8,128)S(1)}, u32[]{:S(2)}, u32[]{:S(2)}) async-start(f32[4,1,6,16,128]{4,3,2,1,0:T(8,128)} %stack.24), calls=%async_computation | async-start | bytes 393216 | tf_op jit(solution)/shard_map/all_to_all | solution.py:15
  42.0 4.5 %all-to-all-done = f32[4,1,6,16,128]{4,3,2,1,0:T(8,128)S(1)} async-done(((f32[4,1,6,16,128]{4,3,2,1,0:T(8,128)}), f32[4,1,6,16,128]{4,3,2,1,0:T(8,128)S(1)}, u32[]{:S(2)}, u32[]{:S(2)}) %all-to-all-start) | async-done | bytes 196640 | tf_op jit(solution)/shard_map/all_to_all | solution.py:15
  46.5 6.4 %all-to-all-start.1 = ((f32[16,32,128]{2,0,1:T(8,128)}), f32[16,32,128]{2,0,1:T(8,128)S(1)}, u32[]{:S(2)}, u32[]{:S(2)}) async-start(f32[16,32,128]{2,0,1:T(8,128)} %copy.69), calls=%async_computation.1 | async-start | bytes 524288 | tf_op jit(solution)/shard_map/all_to_all | solution.py:196
  53.8 7.6 %all-to-all-done.1 = f32[16,32,128]{2,0,1:T(8,128)S(1)} async-done(((f32[16,32,128]{2,0,1:T(8,128)}), f32[16,32,128]{2,0,1:T(8,128)S(1)}, u32[]{:S(2)}, u32[]{:S(2)}) %all-to-all-start.1) | async-done | bytes 262176 | tf_op jit(solution)/shard_map/all_to_all | solution.py:196
  61.4 3.6 %all-to-all-start.2 = ((f32[16,32,128]{2,0,1:T(8,128)}), f32[16,32,128]{2,0,1:T(8,128)S(1)}, u32[]{:S(2)}, u32[]{:S(2)}) async-start(f32[16,32,128]{2,0,1:T(8,128)} %slice.1507), calls=%async_computation.2 | async-start | bytes 524288 | tf_op jit(solution)/shard_map/all_to_all | solution.py:195
  65.3 8.0 %all-to-all-done.2 = f32[16,32,128]{2,0,1:T(8,128)S(1)} async-done(((f32[16,32,128]{2,0,1:T(8,128)}), f32[16,32,128]{2,0,1:T(8,128)S(1)}, u32[]{:S(2)}, u32[]{:S(2)}) %all-to-all-start.2) | async-done | bytes 262176 | tf_op jit(solution)/shard_map/all_to_all | solution.py:195
  77.6 3.6 %all-to-all-start.3 = ((f32[128,4,128]{2,1,0:T(4,128)}), f32[128,4,128]{2,1,0:T(4,128)S(1)}, u32[]{:S(2)}, u32[]{:S(2)}) async-start(f32[128,4,128]{2,1,0:T(4,128)} %copy.76), calls=%async_computation.3 | async-start | bytes 524288 | tf_op jit(solution)/shard_map/all_to_all | solution.py:198
  81.4 8.3 %all-to-all-done.3 = f32[128,4,128]{2,1,0:T(4,128)S(1)} async-done(((f32[128,4,128]{2,1,0:T(4,128)}), f32[128,4,128]{2,1,0:T(4,128)S(1)}, u32[]{:S(2)}, u32[]{:S(2)}) %all-to-all-start.3) | async-done | bytes 262176 | tf_op jit(solution)/shard_map/all_to_all | solution.py:198
  90.8 2.0 fusion.61
  93.8 1.3 collective-permute-start.5
  95.1 4.5 %collective-permute-start.4 = (f32[2,32,128]{2,0,1:T(2,128)S(1)}, f32[2,32,128]{2,0,1:T(2,128)S(1)}, u32[]{:S(2)}, u32[]{:S(2)}) collective-permute-start(f32[2,32,128]{2,0,1:T(2,128)S(1)} %get-tuple-element.1035), channel_id=1, source_target_pairs={{0,4},{4,8},{8,12},{12,16},{16,20},{20,24},{24,28},{1,5},{5,9},{9,... | collective-permute-start | bytes 98312 | tf_op jit(solution)/shard_map/ppermute | solution.py:23
  103.3 1.3 collective-permute-start.7
  105.8 2.8 %collective-permute-done.7 = f32[20,2,128]{2,0,1:T(8,128)S(1)} collective-permute-done((f32[20,2,128]{2,0,1:T(8,128)S(1)}, f32[20,2,128]{2,0,1:T(8,128)S(1)}, u32[]{:S(2)}, u32[]{:S(2)}) %collective-permute-start.7) | collective-permute-done | bytes 20512 | tf_op jit(solution)/shard_map/ppermute | solution.py:26
  110.7 1.7 fusion.26
  120.1 1.3 multiply_add_fusion.35
  128.3 3.8 %all-to-all-start.4 = ((f32[4,1,6,16,128]{4,3,2,1,0:T(8,128)}), f32[4,1,6,16,128]{4,3,2,1,0:T(8,128)S(1)}, u32[]{:S(2)}, u32[]{:S(2)}) async-start(f32[4,1,6,16,128]{4,3,2,1,0:T(8,128)} %stack.27), calls=%async_computation.4 | async-start | bytes 393216 | tf_op jit(solution)/shard_map/all_to_all | solution.py:15
  133.0 4.5 %all-to-all-done.4 = f32[4,1,6,16,128]{4,3,2,1,0:T(8,128)S(1)} async-done(((f32[4,1,6,16,128]{4,3,2,1,0:T(8,128)}), f32[4,1,6,16,128]{4,3,2,1,0:T(8,128)S(1)}, u32[]{:S(2)}, u32[]{:S(2)}) %all-to-all-start.4) | async-done | bytes 196640 | tf_op jit(solution)/shard_map/all_to_all | solution.py:15
  137.4 5.4 %all-to-all-start.5 = ((f32[16,32,128]{2,0,1:T(8,128)}), f32[16,32,128]{2,0,1:T(8,128)S(1)}, u32[]{:S(2)}, u32[]{:S(2)}) async-start(f32[16,32,128]{2,0,1:T(8,128)} %fusion.61), calls=%async_computation.5 | async-start | bytes 524288 | tf_op jit(solution)/shard_map/all_to_all | solution.py:196
  143.7 7.6 %all-to-all-done.5 = f32[16,32,128]{2,0,1:T(8,128)S(1)} async-done(((f32[16,32,128]{2,0,1:T(8,128)}), f32[16,32,128]{2,0,1:T(8,128)S(1)}, u32[]{:S(2)}, u32[]{:S(2)}) %all-to-all-start.5) | async-done | bytes 262176 | tf_op jit(solution)/shard_map/all_to_all | solution.py:196
  151.3 3.6 %all-to-all-start.6 = ((f32[16,32,128]{2,0,1:T(8,128)}), f32[16,32,128]{2,0,1:T(8,128)S(1)}, u32[]{:S(2)}, u32[]{:S(2)}) async-start(f32[16,32,128]{2,0,1:T(8,128)} %slice.1684), calls=%async_computation.6 | async-start | bytes 524288 | tf_op jit(solution)/shard_map/all_to_all | solution.py:195
  155.3 8.0 %all-to-all-done.6 = f32[16,32,128]{2,0,1:T(8,128)S(1)} async-done(((f32[16,32,128]{2,0,1:T(8,128)}), f32[16,32,128]{2,0,1:T(8,128)S(1)}, u32[]{:S(2)}, u32[]{:S(2)}) %all-to-all-start.6) | async-done | bytes 262176 | tf_op jit(solution)/shard_map/all_to_all | solution.py:195
  167.6 3.6 %all-to-all-start.7 = ((f32[128,4,128]{2,1,0:T(4,128)}), f32[128,4,128]{2,1,0:T(4,128)S(1)}, u32[]{:S(2)}, u32[]{:S(2)}) async-start(f32[128,4,128]{2,1,0:T(4,128)} %copy.82), calls=%async_computation.7 | async-start | bytes 524288 | tf_op jit(solution)/shard_map/all_to_all | solution.py:198
  171.4 8.3 %all-to-all-done.7 = f32[128,4,128]{2,1,0:T(4,128)S(1)} async-done(((f32[128,4,128]{2,1,0:T(4,128)}), f32[128,4,128]{2,1,0:T(4,128)S(1)}, u32[]{:S(2)}, u32[]{:S(2)}) %all-to-all-start.7) | async-done | bytes 262176 | tf_op jit(solution)/shard_map/all_to_all | solution.py:198
  180.7 1.3 fusion.54
  183.5 28.7 %all_to_all.123 = f32[16,128,128]{2,1,0:T(8,128)S(1)} all-to-all(f32[16,128,128]{2,1,0:T(8,128)S(1)} %scatter_fusion), channel_id=1, replica_groups=mesh['gz'=8,'xy'=4] {'gz'}, dimensions={0} | all-to-all | bytes 2097152 | tf_op jit(solution)/shard_map/all_to_all | solution.py:213
  (387 shorter events, 58.0 us)
Async XLA Ops:
  3.4 9.4 %collective-permute-start.1 = (f32[2,32,128]{2,0,1:T(2,128)S(1)}, f32[2,32,128]{2,0,1:T(2,128)S(1)}, u32[]{:S(2)}, u32[]{:S(2)}) collective-permute-start(f32[2,32,128]{2,0,1:T(2,128)S(1)} %get-tuple-element.1168), channel_id=1, source_target_pairs={{4,0},{8,4},{12,8},{16,12},{20,16},{24,20},{28,24},{5,1},{9,5},{13... | collective-permute-start | bytes 98312 | tf_op jit(solution)/shard_map/ppermute | solution.py:26
  4.7 8.2 %collective-permute-start = (f32[2,32,128]{2,0,1:T(2,128)S(1)}, f32[2,32,128]{2,0,1:T(2,128)S(1)}, u32[]{:S(2)}, u32[]{:S(2)}) collective-permute-start(f32[2,32,128]{2,0,1:T(2,128)S(1)} %get-tuple-element.1167), channel_id=1, source_target_pairs={{0,4},{4,8},{8,12},{12,16},{16,20},{20,24},{24,28},{1,5},{5,9},{9,... | collective-permute-start | bytes 98312 | tf_op jit(solution)/shard_map/ppermute | solution.py:23
  10.3 14.1 %copy-start.6 = (pred[32]{0:T(512)(128)(4,1)}, pred[32]{0:T(512)(128)(4,1)S(1)}, u32[]{:S(2)}) copy-start(pred[32]{0:T(512)(128)(4,1)S(1)} %get-tuple-element.1185) | copy-start | bytes 100
  11.5 10.1 %copy-start.8 = (pred[34]{0:T(512)(128)(4,1)}, pred[34]{0:T(512)(128)(4,1)S(1)}, u32[]{:S(2)}) copy-start(pred[34]{0:T(512)(128)(4,1)S(1)} %get-tuple-element.1181) | copy-start | bytes 106
  11.5 10.1 %copy-start.10 = (pred[34]{0:T(512)(128)(4,1)}, pred[34]{0:T(512)(128)(4,1)S(1)}, u32[]{:S(2)}) copy-start(pred[34]{0:T(512)(128)(4,1)S(1)} %get-tuple-element.1182) | copy-start | bytes 106
  12.9 8.8 %copy-start.12 = (pred[18]{0:T(512)(128)(4,1)}, pred[18]{0:T(512)(128)(4,1)S(1)}, u32[]{:S(2)}) copy-start(pred[18]{0:T(512)(128)(4,1)S(1)} %get-tuple-element.1183) | copy-start | bytes 58
  12.9 8.8 %copy-start.14 = (pred[18]{0:T(512)(128)(4,1)}, pred[18]{0:T(512)(128)(4,1)S(1)}, u32[]{:S(2)}) copy-start(pred[18]{0:T(512)(128)(4,1)S(1)} %get-tuple-element.1184) | copy-start | bytes 58
  13.7 2.8 %collective-permute-start.2 = (f32[20,2,128]{2,0,1:T(8,128)S(1)}, f32[20,2,128]{2,0,1:T(8,128)S(1)}, u32[]{:S(2)}, u32[]{:S(2)}) collective-permute-start(f32[20,2,128]{2,0,1:T(8,128)S(1)} %get-tuple-element.887), channel_id=1, source_target_pairs={{0,1},{1,2},{2,3},{4,5},{5,6},{6,7},{8,9},{9,10},{10,11},{12,13},{... | collective-permute-start | bytes 61448 | tf_op jit(solution)/shard_map/ppermute | solution.py:23
  15.1 5.1 %collective-permute-start.3 = (f32[20,2,128]{2,0,1:T(8,128)S(1)}, f32[20,2,128]{2,0,1:T(8,128)S(1)}, u32[]{:S(2)}, u32[]{:S(2)}) collective-permute-start(f32[20,2,128]{2,0,1:T(8,128)S(1)} %get-tuple-element.886), channel_id=1, source_target_pairs={{1,0},{2,1},{3,2},{5,4},{6,5},{7,6},{9,8},{10,9},{11,10},{13,12},{... | collective-permute-start | bytes 61448 | tf_op jit(solution)/shard_map/ppermute | solution.py:26
  16.4 7.6 %copy-start.16 = (f32[33]{0:T(128)}, f32[33]{0:T(128)S(1)}, u32[]{:S(2)}) copy-start(f32[33]{0:T(128)S(1)} %fusion.73) | copy-start | bytes 400
  26.2 1.0 copy-start.1
  37.3 9.1 %all-to-all-start = ((f32[4,1,6,16,128]{4,3,2,1,0:T(8,128)}), f32[4,1,6,16,128]{4,3,2,1,0:T(8,128)S(1)}, u32[]{:S(2)}, u32[]{:S(2)}) async-start(f32[4,1,6,16,128]{4,3,2,1,0:T(8,128)} %stack.24), calls=%async_computation | async-start | bytes 393216 | tf_op jit(solution)/shard_map/all_to_all | solution.py:15
  46.5 14.9 %all-to-all-start.1 = ((f32[16,32,128]{2,0,1:T(8,128)}), f32[16,32,128]{2,0,1:T(8,128)S(1)}, u32[]{:S(2)}, u32[]{:S(2)}) async-start(f32[16,32,128]{2,0,1:T(8,128)} %copy.69), calls=%async_computation.1 | async-start | bytes 524288 | tf_op jit(solution)/shard_map/all_to_all | solution.py:196
  61.4 12.0 %all-to-all-start.2 = ((f32[16,32,128]{2,0,1:T(8,128)}), f32[16,32,128]{2,0,1:T(8,128)S(1)}, u32[]{:S(2)}, u32[]{:S(2)}) async-start(f32[16,32,128]{2,0,1:T(8,128)} %slice.1507), calls=%async_computation.2 | async-start | bytes 524288 | tf_op jit(solution)/shard_map/all_to_all | solution.py:195
  77.6 12.1 %all-to-all-start.3 = ((f32[128,4,128]{2,1,0:T(4,128)}), f32[128,4,128]{2,1,0:T(4,128)S(1)}, u32[]{:S(2)}, u32[]{:S(2)}) async-start(f32[128,4,128]{2,1,0:T(4,128)} %copy.76), calls=%async_computation.3 | async-start | bytes 524288 | tf_op jit(solution)/shard_map/all_to_all | solution.py:198
  89.8 1.0 copy-start.3
  89.8 1.0 copy-start.5
  93.8 5.9 %copy-start.20 = (s32[1,4,1]{1,2,0:T(1,128)S(1)}, s32[1,4,1]{1,2,0:T(1,128)}, u32[]{:S(2)}) copy-start(s32[1,4,1]{1,2,0:T(1,128)} %param.11) | copy-start | bytes 52
  93.8 5.9 %copy-start.21 = (s32[4]{0:T(128)S(1)}, s32[4]{0:T(128)}, u32[]{:S(2)}) copy-start(s32[4]{0:T(128)} %convert_reduce_fusion) | copy-start | bytes 52
  93.8 6.4 %collective-permute-start.5 = (f32[2,32,128]{2,0,1:T(2,128)S(1)}, f32[2,32,128]{2,0,1:T(2,128)S(1)}, u32[]{:S(2)}, u32[]{:S(2)}) collective-permute-start(f32[2,32,128]{2,0,1:T(2,128)S(1)} %get-tuple-element.1036), channel_id=1, source_target_pairs={{4,0},{8,4},{12,8},{16,12},{20,16},{24,20},{28,24},{5,1},{9,5},{13... | collective-permute-start | bytes 98312 | tf_op jit(solution)/shard_map/ppermute | solution.py:26
  95.1 6.1 %collective-permute-start.4 = (f32[2,32,128]{2,0,1:T(2,128)S(1)}, f32[2,32,128]{2,0,1:T(2,128)S(1)}, u32[]{:S(2)}, u32[]{:S(2)}) collective-permute-start(f32[2,32,128]{2,0,1:T(2,128)S(1)} %get-tuple-element.1035), channel_id=1, source_target_pairs={{0,4},{4,8},{8,12},{12,16},{16,20},{20,24},{24,28},{1,5},{5,9},{9,... | collective-permute-start | bytes 98312 | tf_op jit(solution)/shard_map/ppermute | solution.py:23
  102.0 3.8 %collective-permute-start.6 = (f32[20,2,128]{2,0,1:T(8,128)S(1)}, f32[20,2,128]{2,0,1:T(8,128)S(1)}, u32[]{:S(2)}, u32[]{:S(2)}) collective-permute-start(f32[20,2,128]{2,0,1:T(8,128)S(1)} %get-tuple-element.885), channel_id=1, source_target_pairs={{0,1},{1,2},{2,3},{4,5},{5,6},{6,7},{8,9},{9,10},{10,11},{12,13},{... | collective-permute-start | bytes 61448 | tf_op jit(solution)/shard_map/ppermute | solution.py:23
  103.3 5.3 %collective-permute-start.7 = (f32[20,2,128]{2,0,1:T(8,128)S(1)}, f32[20,2,128]{2,0,1:T(8,128)S(1)}, u32[]{:S(2)}, u32[]{:S(2)}) collective-permute-start(f32[20,2,128]{2,0,1:T(8,128)S(1)} %get-tuple-element.884), channel_id=1, source_target_pairs={{1,0},{2,1},{3,2},{5,4},{6,5},{7,6},{9,8},{10,9},{11,10},{13,12},{... | collective-permute-start | bytes 61448 | tf_op jit(solution)/shard_map/ppermute | solution.py:26
  110.7 1.7 copy-start.17
  112.5 0.7 copy-start.7
  128.3 9.1 %all-to-all-start.4 = ((f32[4,1,6,16,128]{4,3,2,1,0:T(8,128)}), f32[4,1,6,16,128]{4,3,2,1,0:T(8,128)S(1)}, u32[]{:S(2)}, u32[]{:S(2)}) async-start(f32[4,1,6,16,128]{4,3,2,1,0:T(8,128)} %stack.27), calls=%async_computation.4 | async-start | bytes 393216 | tf_op jit(solution)/shard_map/all_to_all | solution.py:15
  137.4 13.9 %all-to-all-start.5 = ((f32[16,32,128]{2,0,1:T(8,128)}), f32[16,32,128]{2,0,1:T(8,128)S(1)}, u32[]{:S(2)}, u32[]{:S(2)}) async-start(f32[16,32,128]{2,0,1:T(8,128)} %fusion.61), calls=%async_computation.5 | async-start | bytes 524288 | tf_op jit(solution)/shard_map/all_to_all | solution.py:196
  151.3 12.0 %all-to-all-start.6 = ((f32[16,32,128]{2,0,1:T(8,128)}), f32[16,32,128]{2,0,1:T(8,128)S(1)}, u32[]{:S(2)}, u32[]{:S(2)}) async-start(f32[16,32,128]{2,0,1:T(8,128)} %slice.1684), calls=%async_computation.6 | async-start | bytes 524288 | tf_op jit(solution)/shard_map/all_to_all | solution.py:195
  167.6 12.1 %all-to-all-start.7 = ((f32[128,4,128]{2,1,0:T(4,128)}), f32[128,4,128]{2,1,0:T(4,128)S(1)}, u32[]{:S(2)}, u32[]{:S(2)}) async-start(f32[128,4,128]{2,1,0:T(4,128)} %copy.82), calls=%async_computation.7 | async-start | bytes 524288 | tf_op jit(solution)/shard_map/all_to_all | solution.py:198
  179.7 1.0 copy-start.2
  179.7 1.0 copy-start.4
  182.1 0.7 copy-start
  (6 other events, 3.8 us)
